TPU v7x, 32 devices: a whole 2x2x4 slice. The times are simulated.
32 devices in a mesh: dp: 8 (over z, x), tensor: 4 (over y, core).
Axes of the slice: x: 2, y: 2, z: 4, core: 2. Of those that a mesh axis runs over, the one named last changes fastest.
Arguments:
- tokens: bfloat16 [16384, 1024], P(('dp', 'tensor')), may hold values from -6 to 6
- cotangent: bfloat16 [16384, 1024], P(('dp', 'tensor')), may hold values from -6 to 6
- lengths: int32 [8, 16], P('dp'), may hold values from 1 to 256, 2048 in all within a row
- qkv_master: float32 [1024, 3, 1024], P('dp', None, 'tensor'), may hold values from -0.1875 to 0.1875
- qkv_first: float32 [1024, 3, 1024], P('dp', None, 'tensor'), may hold values from -0.00015258789 to 0.00015258789
- qkv_second: float32 [1024, 3, 1024], P('dp', None, 'tensor'), may hold values from 2.9798684e-11 to 4.7677895e-10
- out_master: float32 [1024, 1024], P(('tensor', 'dp')), may hold values from -1 to 1
- out_first: float32 [1024, 1024], P(('tensor', 'dp')), may hold values from -9.1552734e-05 to 9.1552734e-05
- out_second: float32 [1024, 1024], P(('tensor', 'dp')), may hold values from 5.959737e-12 to 9.535579e-11
- in_master: float32 [1024, 2, 4096], P('dp', None, 'tensor'), may hold values from -0.1875 to 0.1875
- in_first: float32 [1024, 2, 4096], P('dp', None, 'tensor'), may hold values from -0.00015258789 to 0.00015258789
- in_second: float32 [1024, 2, 4096], P('dp', None, 'tensor'), may hold values from 2.9798684e-11 to 4.7677895e-10
- down_master: float32 [4096, 1024], P(('tensor', 'dp')), may hold values from -0.09375 to 0.09375
- down_first: float32 [4096, 1024], P(('tensor', 'dp')), may hold values from -0.00015258789 to 0.00015258789
- down_second: float32 [4096, 1024], P(('tensor', 'dp')), may hold values from 2.9798684e-11 to 4.7677895e-10
- norm_gains: float32 [2, 1024], replicated, may hold values from 0.2 to 2.8
- gain_first: float32 [2, 1024], replicated, may hold values from -0.00061035156 to 0.00061035156
- gain_second: float32 [2, 1024], replicated, may hold values from 4.7677895e-10 to 7.628463e-09
Outputs:
- layer_out: bfloat16 [16384, 1024], P(('dp', 'tensor'))
- input_grad: float32 [16384, 1024], P(('dp', 'tensor'))
- qkv_grad: float32 [1024, 3, 1024], P('dp', None, 'tensor')
- qkv_new: float32 [1024, 3, 1024], P('dp', None, 'tensor')
- qkv_first_new: float32 [1024, 3, 1024], P('dp', None, 'tensor')
- qkv_second_new: float32 [1024, 3, 1024], P('dp', None, 'tensor')
- out_grad: float32 [1024, 1024], P(('tensor', 'dp'))
- out_new: float32 [1024, 1024], P(('tensor', 'dp'))
- out_first_new: float32 [1024, 1024], P(('tensor', 'dp'))
- out_second_new: float32 [1024, 1024], P(('tensor', 'dp'))
- in_grad: float32 [1024, 2, 4096], P('dp', None, 'tensor')
- in_new: float32 [1024, 2, 4096], P('dp', None, 'tensor')
- in_first_new: float32 [1024, 2, 4096], P('dp', None, 'tensor')
- in_second_new: float32 [1024, 2, 4096], P('dp', None, 'tensor')
- down_grad: float32 [4096, 1024], P(('tensor', 'dp'))
- down_new: float32 [4096, 1024], P(('tensor', 'dp'))
- down_first_new: float32 [4096, 1024], P(('tensor', 'dp'))
- down_second_new: float32 [4096, 1024], P(('tensor', 'dp'))
- gain_grad: float32 [2, 1024], replicated
- gain_new: float32 [2, 1024], replicated
- gain_first_new: float32 [2, 1024], replicated
- gain_second_new: float32 [2, 1024], replicated
- grad_norm: float32 [], replicated
Inputs may be any that keep to these rules, and one draw needn't show every extreme that they name: Each row's 16 window lengths are positive, add up to 2048, and the longest is 256.
All inputs are finite; a program needn't handle non-finite values.
Results may differ from a plain program's by a relative error of at most 0.024.
Values may be sent and summed in bfloat16 or wider, within the bound.
No kernel may reach another device: no remote copies, remote signals or barrier semaphores. Data moves between devices by JAX's collectives and lax.ppermute only.
A program may use at most 192 MiB of HBM per device.

v0:
```python
from functools import partial
import math
import jax
import jax.numpy as jnp
from jax import lax
from jax.sharding import PartitionSpec as P

D = 1024
HEADS = 16
HEAD_DIM = 64
FF = 4096
ROW = 2048
STEP = 5
eps_norm = 1e-05
beta_one = 0.9
beta_two = 0.999
learn_rate = 0.05
gain_rate = 0.6
weight_decay = 0.1
adam_eps = 1e-08
max_norm = 1.0


def layer_norm(values, gain):
    centre = values - jnp.mean(values, axis=-1, keepdims=True)
    spread = jnp.mean(centre * centre, axis=-1, keepdims=True)
    return centre * lax.rsqrt(spread + eps_norm) * gain


def row_layout(lengths):
    seg_ends = jnp.cumsum(lengths, axis=-1)
    places = jnp.arange(ROW, dtype=jnp.int32)
    passed = (places[:, None] >= seg_ends[..., None, :]).astype(jnp.int32)
    segment = jnp.sum(passed, axis=-1)
    offset = places - jnp.sum(passed * lengths[..., None, :], axis=-1)
    return (segment, offset)


def rotary_tables(offset):
    half_dim = HEAD_DIM // 2
    inverse = jnp.exp(
        jnp.arange(half_dim, dtype=jnp.float32) * (-2.0 * math.log(10000.0) / HEAD_DIM)
    )
    angles = offset.astype(jnp.float32)[..., None] * inverse
    return (jnp.cos(angles), jnp.sin(angles))


def rotate(values, cosine, sine):
    half_dim = values.shape[-1] // 2
    front_half = values[..., :half_dim]
    back_half = values[..., half_dim:]
    cos_wide = cosine[..., None, :]
    sin_wide = sine[..., None, :]
    return jnp.concatenate(
        [
            front_half * cos_wide - back_half * sin_wide,
            back_half * cos_wide + front_half * sin_wide,
        ],
        axis=-1,
    )


def swiglu(gate_up):
    half_cols = gate_up.shape[-1] // 2
    return jax.nn.silu(gate_up[:, :half_cols]) * gate_up[:, half_cols:]


def adam_update(weight, first_moment, second_moment, gradient, factor, use_decay, rate):
    clipped = gradient * factor
    first_new = beta_one * first_moment + (1.0 - beta_one) * clipped
    second_new = beta_two * second_moment + (1.0 - beta_two) * clipped * clipped
    first_hat = first_new / (1.0 - beta_one**STEP)
    second_hat = second_new / (1.0 - beta_two**STEP)
    direction = first_hat / (jnp.sqrt(second_hat) + adam_eps) + use_decay * weight_decay * weight
    return (clipped, weight - rate * direction, first_new, second_new)


def contract_rows(left, right):
    return lax.dot_general(
        left, right, (((0,), (0,)), ((), ())), preferred_element_type=jnp.float32
    )


def contract_cols(left, right):
    return lax.dot_general(
        left, right, (((1,), (1,)), ((), ())), preferred_element_type=jnp.float32
    )


def per_device(
    tokens,
    cotangent,
    lengths,
    qkv_master,
    qkv_first,
    qkv_second,
    out_master,
    out_first,
    out_second,
    in_master,
    in_first,
    in_second,
    down_master,
    down_first,
    down_second,
    norm_gains,
    gain_first,
    gain_second,
):
    heads_local = HEADS // lax.axis_size("tensor")
    width_local = heads_local * HEAD_DIM
    ffn_local = FF // lax.axis_size("tensor")
    row_count = lengths.shape[0]
    all_rows = row_count * ROW
    score_scale = HEAD_DIM ** (-0.5)
    block_rows = min(512, ROW)
    block_count = ROW // block_rows
    w_qkv, w_out, w_in, w_down = (
        lax.all_gather(qkv_master.astype(jnp.bfloat16), "dp", axis=0, tiled=True),
        lax.all_gather(out_master.astype(jnp.bfloat16), "dp", axis=0, tiled=True),
        lax.all_gather(in_master.astype(jnp.bfloat16), "dp", axis=0, tiled=True),
        lax.all_gather(down_master.astype(jnp.bfloat16), "dp", axis=0, tiled=True),
    )
    w_qkv = w_qkv.reshape(D, 3 * width_local)
    w_in = w_in.reshape(D, 2 * ffn_local)
    segment, offset = row_layout(lengths)
    cosine, sine = rotary_tables(offset)
    gain_one = norm_gains[0]
    gain_two = norm_gains[1]
    inputs = tokens.astype(jnp.float32)
    normed = layer_norm(inputs, gain_one)
    gathered_one = lax.all_gather(normed.astype(jnp.bfloat16), "tensor", axis=0, tiled=True)
    projected = jnp.dot(gathered_one, w_qkv, preferred_element_type=jnp.float32)
    projected = projected.reshape(row_count, ROW, 3, heads_local, HEAD_DIM)
    queries = rotate(projected[:, :, 0], cosine, sine).astype(jnp.bfloat16)
    keys = rotate(projected[:, :, 1], cosine, sine).astype(jnp.bfloat16)
    values = projected[:, :, 2].astype(jnp.bfloat16)

    def score_block(query_block, key_row, segment_block, segment_row):
        scores = (
            jnp.einsum("qhd,khd->hqk", query_block, key_row, preferred_element_type=jnp.float32)
            * score_scale
        )
        allowed = segment_block[:, None] == segment_row[None, :]
        return jnp.where(allowed[None], scores, -1e30)

    def forward_row(pieces):
        query_row, key_row, value_row, segment_row = pieces

        def forward_block(block_parts):
            query_block, segment_block = block_parts
            masked = score_block(query_block, key_row, segment_block, segment_row)
            row_max = jnp.max(masked, axis=-1, keepdims=True)
            log_total = (
                jnp.log(jnp.sum(jnp.exp(masked - row_max), axis=-1, keepdims=True)) + row_max
            )
            weights = jnp.exp(masked - log_total).astype(jnp.bfloat16)
            mixed_heads = jnp.einsum(
                "hqk,khd->qhd", weights, value_row, preferred_element_type=jnp.float32
            )
            return (mixed_heads.astype(jnp.bfloat16), log_total)

        return lax.map(
            forward_block,
            (
                query_row.reshape(block_count, block_rows, heads_local, HEAD_DIM),
                segment_row.reshape(block_count, block_rows),
            ),
        )

    mixed_heads, log_totals = lax.map(forward_row, (queries, keys, values, segment))
    attended = mixed_heads.reshape(all_rows, width_local)
    middle = inputs + lax.psum_scatter(
        jnp.dot(attended, w_out, preferred_element_type=jnp.float32),
        "tensor",
        scatter_dimension=0,
        tiled=True,
    )
    normed_two = layer_norm(middle, gain_two)
    gathered_two = lax.all_gather(normed_two.astype(jnp.bfloat16), "tensor", axis=0, tiled=True)
    gate_up = jnp.dot(gathered_two, w_in, preferred_element_type=jnp.float32)
    hidden = swiglu(gate_up).astype(jnp.bfloat16)
    output = middle + lax.psum_scatter(
        jnp.dot(hidden, w_down, preferred_element_type=jnp.float32).astype(jnp.bfloat16),
        "tensor",
        scatter_dimension=0,
        tiled=True,
    ).astype(jnp.float32)
    layer_out = output.astype(jnp.bfloat16)
    upstream = cotangent.astype(jnp.float32)
    gathered_down = lax.all_gather(cotangent, "tensor", axis=0, tiled=True)
    grad_down = contract_rows(hidden, gathered_down)
    hidden_grad = contract_cols(gathered_down, w_down)
    gate_up_grad = jax.vjp(swiglu, gate_up)[1](hidden_grad)[0].astype(jnp.bfloat16)
    grad_in = contract_rows(gathered_two, gate_up_grad)
    normed_two_grad = lax.psum_scatter(
        contract_cols(gate_up_grad, w_in).astype(jnp.bfloat16),
        "tensor",
        scatter_dimension=0,
        tiled=True,
    ).astype(jnp.float32)
    middle_back, gain_two_grad = jax.vjp(layer_norm, middle, gain_two)[1](normed_two_grad)
    middle_grad = upstream + middle_back
    gathered_mid = lax.all_gather(middle_grad.astype(jnp.bfloat16), "tensor", axis=0, tiled=True)
    grad_out = contract_rows(attended, gathered_mid)
    attended_grad = contract_cols(gathered_mid, w_out).astype(jnp.bfloat16)
    attended_grad = attended_grad.reshape(row_count, ROW, heads_local, HEAD_DIM)

    def backward_row(pieces):
        query_row, key_row, value_row, segment_row, total_row, grad_row = pieces

        def backward_block(running, block_parts):
            key_acc, value_acc = running
            query_block, segment_block, total_block, grad_block = block_parts
            masked = score_block(query_block, key_row, segment_block, segment_row)
            probs_block = jnp.exp(masked - total_block)
            probs_low = probs_block.astype(jnp.bfloat16)
            prob_grad = jnp.einsum(
                "qhd,khd->hqk", grad_block, value_row, preferred_element_type=jnp.float32
            )
            row_inner = jnp.sum(probs_block * prob_grad, axis=-1, keepdims=True)
            score_grad = (probs_block * (prob_grad - row_inner)).astype(jnp.bfloat16)
            query_grad = (
                jnp.einsum("hqk,khd->qhd", score_grad, key_row, preferred_element_type=jnp.float32)
                * score_scale
            )
            key_acc = (
                key_acc
                + jnp.einsum(
                    "hqk,qhd->khd", score_grad, query_block, preferred_element_type=jnp.float32
                )
                * score_scale
            )
            value_acc = value_acc + jnp.einsum(
                "hqk,qhd->khd", probs_low, grad_block, preferred_element_type=jnp.float32
            )
            return ((key_acc, value_acc), query_grad)

        zeros_acc = jnp.zeros((ROW, heads_local, HEAD_DIM), jnp.float32)
        block_inputs = (
            query_row.reshape(block_count, block_rows, heads_local, HEAD_DIM),
            segment_row.reshape(block_count, block_rows),
            total_row,
            grad_row.reshape(block_count, block_rows, heads_local, HEAD_DIM),
        )
        (key_grad, value_grad), query_grad = lax.scan(
            backward_block, (zeros_acc, zeros_acc), block_inputs
        )
        return (query_grad.reshape(ROW, heads_local, HEAD_DIM), key_grad, value_grad)

    query_grad, key_grad, value_grad = lax.map(
        backward_row, (queries, keys, values, segment, log_totals, attended_grad)
    )
    rotate_back = jax.vjp(partial(rotate, cosine=cosine, sine=sine), projected[:, :, 0])[1]
    query_raw = rotate_back(query_grad)[0]
    key_raw = rotate_back(key_grad)[0]
    qkv_grad_low = (
        jnp.stack([query_raw, key_raw, value_grad], axis=2)
        .reshape(all_rows, 3 * width_local)
        .astype(jnp.bfloat16)
    )
    grad_qkv = contract_rows(gathered_one, qkv_grad_low)
    normed_grad = lax.psum_scatter(
        contract_cols(qkv_grad_low, w_qkv).astype(jnp.bfloat16),
        "tensor",
        scatter_dimension=0,
        tiled=True,
    ).astype(jnp.float32)
    input_back, gain_one_grad = jax.vjp(layer_norm, inputs, gain_one)[1](normed_grad)
    input_grad = middle_grad + input_back
    reduced_qkv, reduced_out, reduced_in, reduced_down = (
        lax.psum_scatter(
            grad_qkv.reshape(D, 3, width_local).astype(jnp.bfloat16),
            "dp",
            scatter_dimension=0,
            tiled=True,
        ).astype(jnp.float32),
        lax.psum_scatter(
            grad_out.astype(jnp.bfloat16), "dp", scatter_dimension=0, tiled=True
        ).astype(jnp.float32),
        lax.psum_scatter(
            grad_in.reshape(D, 2, ffn_local).astype(jnp.bfloat16),
            "dp",
            scatter_dimension=0,
            tiled=True,
        ).astype(jnp.float32),
        lax.psum_scatter(
            grad_down.astype(jnp.bfloat16), "dp", scatter_dimension=0, tiled=True
        ).astype(jnp.float32),
    )
    local_squares = (
        jnp.sum(reduced_qkv * reduced_qkv)
        + jnp.sum(reduced_out * reduced_out)
        + jnp.sum(reduced_in * reduced_in)
        + jnp.sum(reduced_down * reduced_down)
    )
    gain_part = jnp.stack([gain_one_grad, gain_two_grad])
    gain_total, weight_squares = lax.psum((gain_part, local_squares), ("dp", "tensor"))
    grad_norm = jnp.sqrt(weight_squares + jnp.sum(gain_total * gain_total))
    factor = max_norm / jnp.maximum(grad_norm, max_norm)
    qkv_res = adam_update(qkv_master, qkv_first, qkv_second, reduced_qkv, factor, 1.0, learn_rate)
    out_res = adam_update(out_master, out_first, out_second, reduced_out, factor, 1.0, learn_rate)
    in_res = adam_update(in_master, in_first, in_second, reduced_in, factor, 1.0, learn_rate)
    down_res = adam_update(
        down_master, down_first, down_second, reduced_down, factor, 1.0, learn_rate
    )
    gain_res = adam_update(norm_gains, gain_first, gain_second, gain_total, factor, 0.0, gain_rate)
    return (
        layer_out,
        input_grad,
        qkv_res[0],
        qkv_res[1],
        qkv_res[2],
        qkv_res[3],
        out_res[0],
        out_res[1],
        out_res[2],
        out_res[3],
        in_res[0],
        in_res[1],
        in_res[2],
        in_res[3],
        down_res[0],
        down_res[1],
        down_res[2],
        down_res[3],
        gain_res[0],
        gain_res[1],
        gain_res[2],
        gain_res[3],
        grad_norm,
    )


def solution(mesh):
    placed = (
        P(("dp", "tensor"), None),
        P(("dp", "tensor"), None),
        P("dp", None),
        P("dp", None, "tensor"),
        P("dp", None, "tensor"),
        P("dp", None, "tensor"),
        P(("tensor", "dp"), None),
        P(("tensor", "dp"), None),
        P(("tensor", "dp"), None),
        P("dp", None, "tensor"),
        P("dp", None, "tensor"),
        P("dp", None, "tensor"),
        P(("tensor", "dp"), None),
        P(("tensor", "dp"), None),
        P(("tensor", "dp"), None),
        P(),
        P(),
        P(),
    )
    return jax.shard_map(
        per_device,
        mesh=mesh,
        in_specs=placed,
        out_specs=(
            P(("dp", "tensor"), None),
            P(("dp", "tensor"), None),
            P("dp", None, "tensor"),
            P("dp", None, "tensor"),
            P("dp", None, "tensor"),
            P("dp", None, "tensor"),
            P(("tensor", "dp"), None),
            P(("tensor", "dp"), None),
            P(("tensor", "dp"), None),
            P(("tensor", "dp"), None),
            P("dp", None, "tensor"),
            P("dp", None, "tensor"),
            P("dp", None, "tensor"),
            P("dp", None, "tensor"),
            P(("tensor", "dp"), None),
            P(("tensor", "dp"), None),
            P(("tensor", "dp"), None),
            P(("tensor", "dp"), None),
            P(),
            P(),
            P(),
            P(),
            P(),
        ),
        check_vma=False,
    )
```

profile of v0, /device:TPU:0, one launch (start us, length us, event | category | flops | bytes accessed | tf_op | source)
XLA Modules:
  0.0 1104.4 jit_solution(1875028781626215786)
XLA Ops:
  16.8 36.3 %all_gather.26 = bf16[256,1024]{1,0:T(8,128)(2,1)} all-gather(bf16[32,1024]{1,0:T(8,128)(2,1)S(1)} %convert_element_type.159), channel_id=1, replica_groups=mesh['dp'=8,'tensor'=4] {'dp'}, dimensions={0}, use_global_device_ids=true | all-gather | bytes 589824 | tf_op jit(solution)/shard_map/all_gather | solution.py:120
  61.6 35.9 %all-gather.8.cloned.1.call-done = bf16[2048,1024]{1,0:T(8,128)(2,1)} async-done(((bf16[512,1024]{1,0:T(8,128)(2,1)}), bf16[2048,1024]{1,0:T(8,128)(2,1)}) %all-gather.8.cloned.1.call-update) | async-done | bytes 4194320 | tf_op jit(solution)/shard_map/all_gather | solution.py:132
  110.1 57.2 %while.47 = (s32[]{:T(128)}, bf16[4,512,4,64]{1,3,2,0:T(8,128)(2,1)}, f32[4,4,512,1]{2,1,3,0:T(4,128)}, s32[4,512]{1,0:T(4,128)S(1)}, s32[2048]{0:T(1024)S(1)}, ...) while((s32[]{:T(128)}, ...), condition=%wide.region_8.9_spmd, body=%wide.region_5.8_spmd.sunk | while | flops 1121056768 | bytes 57227380 | solution.py:163
  178.4 69.5 %reduce-scatter.8.cloned.1.call-done = f32[512,1024]{1,0:T(8,128)} async-done(((f32[2048,1024]{1,0:T(8,128)}), f32[512,1024]{1,0:T(8,128)}) %reduce-scatter.8.cloned.1.call-update) | async-done | bytes 2097168 | tf_op jit(solution)/shard_map/reduce_scatter | solution.py:173
  254.4 69.7 %all-gather.14.cloned.1.call-done = bf16[1024,2,1024]{2,1,0:T(2,128)(2,1)} async-done(((bf16[128,2,1024]{2,1,0:T(2,128)(2,1)}), bf16[1024,2,1024]{2,1,0:T(2,128)(2,1)}) %all-gather.14.cloned.1.call-update) | async-done | bytes 4194320 | tf_op jit(solution)/shard_map/all_gather | solution.py:121
  329.7 29.2 %all-gather.12.cloned.1.call-done = bf16[2048,1024]{1,0:T(8,128)(2,1)} async-done(((bf16[512,1024]{1,0:T(8,128)(2,1)}), bf16[2048,1024]{1,0:T(8,128)(2,1)}) %all-gather.12.cloned.1.call-update) | async-done | bytes 4194320 | tf_op jit(solution)/shard_map/all_gather | solution.py:180
  358.9 15.1 %fusion.96 = f32[2048,2048]{1,0:T(8,128)} fusion(bf16[2048,1024]{1,0:T(8,128)(2,1)} %all-gather.12.cloned.1.call-done, bf16[1024,2048]{1,0:T(8,128)(2,1)} %bitcast.176), kind=kOutput, calls=%fused_computation.180 | convolution fusion | flops 8589934592 | bytes 25165824 | tf_op jit(solution)/shard_map/dot_general | solution.py:181
  374.0 37.0 %all-gather.16.cloned.1.call-done = bf16[1024,1024]{1,0:T(8,128)(2,1)} async-done(((bf16[128,1024]{1,0:T(8,128)(2,1)}), bf16[1024,1024]{1,0:T(8,128)(2,1)}) %all-gather.16.cloned.1.call-update) | async-done | bytes 2097168 | tf_op jit(solution)/shard_map/all_gather | solution.py:122
  411.0 34.6 %all-gather.18.cloned.1.call-done = bf16[2048,1024]{1,0:T(8,128)(2,1)} async-done(((bf16[512,1024]{1,0:T(8,128)(2,1)}), bf16[2048,1024]{1,0:T(8,128)(2,1)}) %all-gather.18.cloned.1.call-update) | async-done | bytes 4194320 | tf_op jit(solution)/shard_map/all_gather | solution.py:191
  445.6 17.2 %fusion.73 = (f32[2048,1024]{1,0:T(8,128)}, f32[2048,1024]{1,0:T(8,128)}, bf16[2048,1024]{1,0:T(8,128)(2,1)}) fusion(f32[2048,2048]{1,0:T(8,128)} %fusion.96, bf16[2048,1024]{1,0:T(8,128)(2,1)} %all-gather.18.cloned.1.call-done, bf16[1024,1024]{1,0:T(8,128)(2,1)} %all-gather.16.cloned.1.call-done), kind=kOutput, calls=%fused_computation.124 | convolution fusion | flops 4324327424 | bytes 44040192 | tf_op jit(solution)/shard_map/dot_general | solution.py:85
  462.8 15.0 %convolution_convert_fusion.1 = bf16[2048,1024]{1,0:T(8,128)(2,1)} fusion(bf16[1024,2048]{1,0:T(8,128)(2,1)} %bitcast.177, f32[2048,1024]{1,0:T(8,128)} %get-tuple-element.338, f32[2048,1024]{1,0:T(8,128)} %get-tuple-element.337), kind=kOutput, calls=%fused_computation.65 | convolution fusion | flops 8600420352 | bytes 25165824 | tf_op jit(solution)/shard_map/dot_general | solution.py:85
  478.4 9.6 convolution_convert_fusion.3
  488.0 34.6 %reduce-scatter.12.cloned.1.call-done = bf16[512,1024]{1,0:T(8,128)(2,1)} async-done(((bf16[2048,1024]{1,0:T(8,128)(2,1)}), bf16[512,1024]{1,0:T(8,128)(2,1)}) %reduce-scatter.12.cloned.1.call-update) | async-done | bytes 1048592 | tf_op jit(solution)/shard_map/reduce_scatter | solution.py:196
  525.3 44.4 %reduce-scatter.10.cloned.1.call-done = bf16[512,1024]{1,0:T(8,128)(2,1)} async-done(((bf16[2048,1024]{1,0:T(8,128)(2,1)}), bf16[512,1024]{1,0:T(8,128)(2,1)}) %reduce-scatter.10.cloned.1.call-update) | async-done | bytes 1048592 | tf_op jit(solution)/shard_map/reduce_scatter | solution.py:183
  575.8 17.0 %convolution_convert_fusion = bf16[1024,2048]{1,0:T(8,128)(2,1)} fusion(bf16[2048,1024]{1,0:T(8,128)(2,1)} %all-gather.12.cloned.1.call-done, f32[2048,1024]{1,0:T(8,128)} %get-tuple-element.338, f32[2048,1024]{1,0:T(8,128)} %get-tuple-element.337), kind=kOutput, calls=%fused_computation.64 | convolution fusion | flops 8600420352 | bytes 25165824 | tf_op jit(solution)/shard_map/dot_general | solution.py:79
  620.5 230.1 %while.48 = (s32[]{:T(128)}, f32[2048,4,64]{0,2,1:T(8,128)}, f32[2048,4,64]{0,2,1:T(8,128)}, f32[4,512,4,64]{1,0,3,2:T(4,128)}, bf16[4,512,4,64]{1,3,2,0:T(8,128...) while((s32[]{:T(128)}, f32[2048,4,64]{0,2,1:T(8,128)}, ...), condition=%wide.region_18.19_spmd.clone, body=%wide.region_16.18_spmd.clone.sunk | while | flops 2751068160 | bytes 183179600 | solution.py:246
  632.8 11.5 %multiply_reduce_fusion.4 = (f32[4,512]{1,0:T(4,128)}, f32[4,512,2048]{2,1,0:T(8,128)}) fusion(f32[4,512,2048]{2,1,0:T(8,128)S(1)} %fusion.154, f32[4,512]{1,0:T(4,128)S(1)} %dynamic-slice_bitcast_fusion.2, pred[512,2048]{1,0:T(8,128)(4,1)} %copy-done.1, bf16[2048,4,64]{0,2,1:T(8,128)(2,1)} %get-tuple-element.552, ...), kind=kOutput, calls=%fused_computation.20.clone.1 | convolution fusion | flops 557840384 | bytes 35930116 | tf_op jit(solution)/shard_map/while/body/eval_jaxpr/while/body/eval_jaxpr/qhd,khd->hqk/dot_general | solution.py:218
  644.4 11.2 %multiply_convert_fusion.4 = bf16[4,512,2048]{2,1,0:T(8,128)(2,1)} fusion(f32[4,512,2048]{2,1,0:T(8,128)} %get-tuple-element.487, f32[4,512,2048]{2,1,0:T(8,128)S(1)} %fusion.154, f32[4,512]{1,0:T(4,128)} %get-tuple-element.488, f32[4,512]{1,0:T(4,128)S(1)} %dynamic-slice_bitcast_fusion.2, pred[512,2048]{1,0:T(8,128)(4,1)} %copy-done.1), kind=kLoop, calls=%fused_computation.19.clone.1 | loop fusion | flops 25165824 | bytes 43008000 | tf_op jit(solution)/shard_map/while/body/eval_jaxpr/while/body/eval_jaxpr/convert_element_type | solution.py:222
  666.2 11.1 %dynamic_update_slice.33 = f32[4,512,4,64]{1,0,3,2:T(4,128)} dynamic-update-slice(f32[4,512,4,64]{1,0,3,2:T(4,128)} %get-tuple-element.532, f32[1,512,4,64]{1,0,3,2:T(1,128)S(1)} %copy.107, s32[]{:T(128)S(6)} %copy.125, s32[]{:T(128)} %constant.79.clone.1..sunk, s32[]{:T(128)} %constant.79.clone.1..sunk, s32[]{:T(128)} %constant.79.clone.1..sunk) | dynamic-update-slice | bytes 1048580 | tf_op jit(solution)/shard_map/while/body/eval_jaxpr/while/body/jit(dynamic_update_index_in_dim)/dynamic_update_slice | solution.py:246
  689.9 11.5 %multiply_reduce_fusion.4 = (f32[4,512]{1,0:T(4,128)}, f32[4,512,2048]{2,1,0:T(8,128)}) fusion(f32[4,512,2048]{2,1,0:T(8,128)S(1)} %fusion.154, f32[4,512]{1,0:T(4,128)S(1)} %dynamic-slice_bitcast_fusion.2, pred[512,2048]{1,0:T(8,128)(4,1)} %copy-done.1, bf16[2048,4,64]{0,2,1:T(8,128)(2,1)} %get-tuple-element.552, ...), kind=kOutput, calls=%fused_computation.20.clone.1 | convolution fusion | flops 557840384 | bytes 35930116 | tf_op jit(solution)/shard_map/while/body/eval_jaxpr/while/body/eval_jaxpr/qhd,khd->hqk/dot_general | solution.py:218
  701.4 11.0 %multiply_convert_fusion.4 = bf16[4,512,2048]{2,1,0:T(8,128)(2,1)} fusion(f32[4,512,2048]{2,1,0:T(8,128)} %get-tuple-element.487, f32[4,512,2048]{2,1,0:T(8,128)S(1)} %fusion.154, f32[4,512]{1,0:T(4,128)} %get-tuple-element.488, f32[4,512]{1,0:T(4,128)S(1)} %dynamic-slice_bitcast_fusion.2, pred[512,2048]{1,0:T(8,128)(4,1)} %copy-done.1), kind=kLoop, calls=%fused_computation.19.clone.1 | loop fusion | flops 25165824 | bytes 43008000 | tf_op jit(solution)/shard_map/while/body/eval_jaxpr/while/body/eval_jaxpr/convert_element_type | solution.py:222
  723.9 11.1 %dynamic_update_slice.33 = f32[4,512,4,64]{1,0,3,2:T(4,128)} dynamic-update-slice(f32[4,512,4,64]{1,0,3,2:T(4,128)} %get-tuple-element.532, f32[1,512,4,64]{1,0,3,2:T(1,128)S(1)} %copy.107, s32[]{:T(128)S(6)} %copy.125, s32[]{:T(128)} %constant.79.clone.1..sunk, s32[]{:T(128)} %constant.79.clone.1..sunk, s32[]{:T(128)} %constant.79.clone.1..sunk) | dynamic-update-slice | bytes 1048580 | tf_op jit(solution)/shard_map/while/body/eval_jaxpr/while/body/jit(dynamic_update_index_in_dim)/dynamic_update_slice | solution.py:246
  747.6 11.5 %multiply_reduce_fusion.4 = (f32[4,512]{1,0:T(4,128)}, f32[4,512,2048]{2,1,0:T(8,128)}) fusion(f32[4,512,2048]{2,1,0:T(8,128)S(1)} %fusion.154, f32[4,512]{1,0:T(4,128)S(1)} %dynamic-slice_bitcast_fusion.2, pred[512,2048]{1,0:T(8,128)(4,1)} %copy-done.1, bf16[2048,4,64]{0,2,1:T(8,128)(2,1)} %get-tuple-element.552, ...), kind=kOutput, calls=%fused_computation.20.clone.1 | convolution fusion | flops 557840384 | bytes 35930116 | tf_op jit(solution)/shard_map/while/body/eval_jaxpr/while/body/eval_jaxpr/qhd,khd->hqk/dot_general | solution.py:218
  759.2 11.0 multiply_convert_fusion.4
  781.6 11.1 %dynamic_update_slice.33 = f32[4,512,4,64]{1,0,3,2:T(4,128)} dynamic-update-slice(f32[4,512,4,64]{1,0,3,2:T(4,128)} %get-tuple-element.532, f32[1,512,4,64]{1,0,3,2:T(1,128)S(1)} %copy.107, s32[]{:T(128)S(6)} %copy.125, s32[]{:T(128)} %constant.79.clone.1..sunk, s32[]{:T(128)} %constant.79.clone.1..sunk, s32[]{:T(128)} %constant.79.clone.1..sunk) | dynamic-update-slice | bytes 1048580 | tf_op jit(solution)/shard_map/while/body/eval_jaxpr/while/body/jit(dynamic_update_index_in_dim)/dynamic_update_slice | solution.py:246
  805.3 11.5 %multiply_reduce_fusion.4 = (f32[4,512]{1,0:T(4,128)}, f32[4,512,2048]{2,1,0:T(8,128)}) fusion(f32[4,512,2048]{2,1,0:T(8,128)S(1)} %fusion.154, f32[4,512]{1,0:T(4,128)S(1)} %dynamic-slice_bitcast_fusion.2, pred[512,2048]{1,0:T(8,128)(4,1)} %copy-done.1, bf16[2048,4,64]{0,2,1:T(8,128)(2,1)} %get-tuple-element.552, ...), kind=kOutput, calls=%fused_computation.20.clone.1 | convolution fusion | flops 557840384 | bytes 35930116 | tf_op jit(solution)/shard_map/while/body/eval_jaxpr/while/body/eval_jaxpr/qhd,khd->hqk/dot_general | solution.py:218
  816.8 11.0 multiply_convert_fusion.4
  839.3 11.1 %dynamic_update_slice.33 = f32[4,512,4,64]{1,0,3,2:T(4,128)} dynamic-update-slice(f32[4,512,4,64]{1,0,3,2:T(4,128)} %get-tuple-element.532, f32[1,512,4,64]{1,0,3,2:T(1,128)S(1)} %copy.107, s32[]{:T(128)S(6)} %copy.125, s32[]{:T(128)} %constant.79.clone.1..sunk, s32[]{:T(128)} %constant.79.clone.1..sunk, s32[]{:T(128)} %constant.79.clone.1..sunk) | dynamic-update-slice | bytes 1048580 | tf_op jit(solution)/shard_map/while/body/eval_jaxpr/while/body/jit(dynamic_update_index_in_dim)/dynamic_update_slice | solution.py:246
  883.5 37.6 %reduce-scatter.18.cloned.1.call-done = bf16[32,1024]{1,0:T(8,128)(2,1)} async-done(((bf16[256,1024]{1,0:T(8,128)(2,1)}), bf16[32,1024]{1,0:T(8,128)(2,1)}) %reduce-scatter.18.cloned.1.call-update) | async-done | bytes 65552 | tf_op jit(solution)/shard_map/reduce_scatter | solution.py:278
  922.6 66.9 %reduce-scatter.16.cloned.1.call-done = bf16[128,3,256]{2,0,1:T(8,128)(2,1)} async-done(((bf16[1024,3,256]{2,0,1:T(8,128)(2,1)}), bf16[128,3,256]{2,0,1:T(8,128)(2,1)}) %reduce-scatter.16.cloned.1.call-update) | async-done | bytes 196624 | tf_op jit(solution)/shard_map/reduce_scatter | solution.py:272
  993.7 41.8 %reduce-scatter.14.cloned.1.call-done = bf16[512,1024]{1,0:T(8,128)(2,1)} async-done(((bf16[2048,1024]{1,0:T(8,128)(2,1)}), bf16[512,1024]{1,0:T(8,128)(2,1)}) %reduce-scatter.14.cloned.1.call-update) | async-done | bytes 1048592 | tf_op jit(solution)/shard_map/reduce_scatter | solution.py:263
  1039.7 39.7 %all-reduce.7 = (f32[]{:T(128)}, f32[2,1024]{1,0:T(2,128)S(1)}) all-reduce(f32[]{:T(128)S(6)} %add.210, f32[2,1024]{1,0:T(2,128)S(1)} %pad_maximum_fusion.1), channel_id=1, replica_groups=mesh['dp'=8,'tensor'=4] {'dp','tensor'}, use_global_device_ids=true, to_apply=%region_30.31 | all-reduce | flops 2049 | bytes 16392 | tf_op jit(solution)/shard_map/psum | solution.py:298
  (313 shorter events, 297.0 us)
Async XLA Ops:
  7.2 54.4 %all-gather.10.cloned.1.call-start = ((), (), s32[]{:S(2)}) async-start(), calls=%async_computation.8 | async-start | bytes 1769472 | tf_op jit(solution)/shard_map/all_gather | solution.py:119
  9.1 88.4 %all-gather.8.cloned.1.call-start = ((), (), s32[]{:S(2)}) async-start(), calls=%async_computation.7 | async-start | bytes 5242880 | tf_op jit(solution)/shard_map/all_gather | solution.py:132
  16.3 231.6 %reduce-scatter.8.cloned.1.call-start = ((), (), s32[]{:S(2)}) async-start(), calls=%async_computation.9 | async-start | bytes 10485760 | tf_op jit(solution)/shard_map/reduce_scatter | solution.py:173
  54.1 50.3 %copy-start.14 = (f32[2048,32]{0,1:T(8,128)}, f32[2048,32]{0,1:T(8,128)S(1)}, u32[]{:S(2)}) copy-start(f32[2048,32]{0,1:T(8,128)S(1)} %get-tuple-element.355) | copy-start | bytes 786436
  54.1 50.3 %copy-start.16 = (f32[2048,32]{0,1:T(8,128)}, f32[2048,32]{0,1:T(8,128)S(1)}, u32[]{:S(2)}) copy-start(f32[2048,32]{0,1:T(8,128)S(1)} %get-tuple-element.356) | copy-start | bytes 786436
  176.0 148.1 %all-gather.14.cloned.1.call-start = ((), (), s32[]{:S(2)}) async-start(), calls=%async_computation.11 | async-start | bytes 4718592 | tf_op jit(solution)/shard_map/all_gather | solution.py:121
  178.4 180.5 %all-gather.12.cloned.1.call-start = ((), (), s32[]{:S(2)}) async-start(), calls=%async_computation.10 | async-start | bytes 5242880 | tf_op jit(solution)/shard_map/all_gather | solution.py:180
  251.7 159.3 %all-gather.16.cloned.1.call-start = ((), (), s32[]{:S(2)}) async-start(), calls=%async_computation.12 | async-start | bytes 2359296 | tf_op jit(solution)/shard_map/all_gather | solution.py:122
  253.6 192.1 %all-gather.18.cloned.1.call-start = ((), (), s32[]{:S(2)}) async-start(), calls=%async_computation.14 | async-start | bytes 5242880 | tf_op jit(solution)/shard_map/all_gather | solution.py:191
  254.3 268.3 %reduce-scatter.12.cloned.1.call-start = ((), (), s32[]{:S(2)}) async-start(), calls=%async_computation.15 | async-start | bytes 5242880 | tf_op jit(solution)/shard_map/reduce_scatter | solution.py:196
  477.9 91.8 %reduce-scatter.10.cloned.1.call-start = ((), (), s32[]{:S(2)}) async-start(), calls=%async_computation.13 | async-start | bytes 5242880 | tf_op jit(solution)/shard_map/reduce_scatter | solution.py:183
  488.0 122.4 %all-gather.20.cloned.1.call-start = ((), (), s32[]{:S(2)}) async-start(), calls=%async_computation.16 | async-start | bytes 5242880 | tf_op jit(solution)/shard_map/all_gather | solution.py:204
  573.1 19.7 %copy-start.45 = (f32[512]{0:T(512)}, f32[512]{0:T(512)S(1)}, u32[]{:S(2)}) copy-start(f32[512]{0:T(512)S(1)} %negate_multiply_fusion.1) | copy-start | bytes 6148
  575.7 303.3 %all-reduce.10.cloned.1.call-start = ((), (), s32[]{:S(2)}) async-start(), calls=%async_computation.21 | async-start | bytes 8388608
  600.7 281.1 %reduce-scatter.20.cloned.1.call-start = ((), (), s32[]{:S(2)}) async-start(), calls=%async_computation.20 | async-start | bytes 2359296 | tf_op jit(solution)/shard_map/reduce_scatter | solution.py:287
  610.3 310.8 %reduce-scatter.18.cloned.1.call-start = ((), (), s32[]{:S(2)}) async-start(), calls=%async_computation.19 | async-start | bytes 589824 | tf_op jit(solution)/shard_map/reduce_scatter | solution.py:278
  718.7 16.4 %copy-start.22 = (s32[2048]{0:T(1024)S(1)}, s32[2048]{0:T(1024)}, u32[]{:S(2)}) copy-start(s32[2048]{0:T(1024)} %copy-done.21) | copy-start | bytes 24580 | tf_op jit(solution)/shard_map/while/body/eval_jaxpr/while
  718.7 16.4 %copy-start.39 = (s32[4,512]{1,0:T(4,128)S(1)}, s32[4,512]{1,0:T(4,128)}, u32[]{:S(2)}) copy-start(s32[4,512]{1,0:T(4,128)} %copy-done.38) | copy-start | bytes 24580 | tf_op jit(solution)/shard_map/while/body/eval_jaxpr/while
  776.4 16.3 %copy-start.22 = (s32[2048]{0:T(1024)S(1)}, s32[2048]{0:T(1024)}, u32[]{:S(2)}) copy-start(s32[2048]{0:T(1024)} %copy-done.21) | copy-start | bytes 24580 | tf_op jit(solution)/shard_map/while/body/eval_jaxpr/while
  858.7 130.7 %reduce-scatter.16.cloned.1.call-start = ((), (), s32[]{:S(2)}) async-start(), calls=%async_computation.18 | async-start | bytes 1769472 | tf_op jit(solution)/shard_map/reduce_scatter | solution.py:272
  870.1 165.4 %reduce-scatter.14.cloned.1.call-start = ((), (), s32[]{:S(2)}) async-start(), calls=%async_computation.17 | async-start | bytes 5242880 | tf_op jit(solution)/shard_map/reduce_scatter | solution.py:263
  877.2 158.3 %copy-start.3 = (bf16[512,1024]{1,0:T(8,128)(2,1)S(1)}, bf16[512,1024]{1,0:T(8,128)(2,1)}, u32[]{:S(2)}) copy-start(bf16[512,1024]{1,0:T(8,128)(2,1)} %param.22) | copy-start | bytes 3145732
  877.2 158.3 %copy-start.37 = (f32[1,1024]{1,0:T(1,128)S(1)}, f32[1,1024]{1,0:T(1,128)}, u32[]{:S(2)}) copy-start(f32[1,1024]{1,0:T(1,128)} %copy-done.36) | copy-start | bytes 12292
  877.2 158.3 %copy-start.41 = (f32[512]{0:T(512)S(1)}, f32[512]{0:T(512)}, u32[]{:S(2)}) copy-start(f32[512]{0:T(512)} %copy-done.40) | copy-start | bytes 6148
  877.2 160.1 %copy-start.48 = (f32[512]{0:T(512)S(1)}, f32[512]{0:T(512)}, u32[]{:S(2)}) copy-start(f32[512]{0:T(512)} %copy-done.47) | copy-start | bytes 6148
  877.2 160.1 %copy-start.44 = (f32[512]{0:T(512)S(1)}, f32[512]{0:T(512)}, u32[]{:S(2)}) copy-start(f32[512]{0:T(512)} %copy-done.43) | copy-start | bytes 6148
  877.2 162.5 %copy-start.49 = (f32[1024]{0:T(1024)S(1)}, f32[1024]{0:T(1024)}, u32[]{:S(2)}) copy-start(f32[1024]{0:T(1024)} %get-tuple-element.261) | copy-start | bytes 12292
  877.2 204.3 %copy-start.42 = (f32[2,1024]{1,0:T(2,128)S(1)}, f32[2,1024]{1,0:T(2,128)}, u32[]{:S(2)}) copy-start(f32[2,1024]{1,0:T(2,128)} %param.37) | copy-start | bytes 24580
  877.2 204.3 %copy-start.50 = (f32[2,1024]{1,0:T(2,128)S(1)}, f32[2,1024]{1,0:T(2,128)}, u32[]{:S(2)}) copy-start(f32[2,1024]{1,0:T(2,128)} %param.38) | copy-start | bytes 24580
  877.2 204.3 %copy-start.51 = (f32[2,1024]{1,0:T(2,128)S(1)}, f32[2,1024]{1,0:T(2,128)}, u32[]{:S(2)}) copy-start(f32[2,1024]{1,0:T(2,128)} %param.39) | copy-start | bytes 24580
  877.3 204.9 %copy-start.7 = (f32[512,1024]{1,0:T(8,128)S(1)}, f32[512,1024]{1,0:T(8,128)}, u32[]{:S(2)}) copy-start(f32[512,1024]{1,0:T(8,128)} %copy-done.6) | copy-start | bytes 6291460
  877.3 204.9 %copy-start.46 = (f32[512]{0:T(512)S(1)}, f32[512]{0:T(512)}, u32[]{:S(2)}) copy-start(f32[512]{0:T(512)} %copy-done.45) | copy-start | bytes 6148
  (57 other events, 324.8 us)
Sparse Core Ops, SparseCore 0:
  10.7 50.9 all-gather.9
  63.8 33.7 all-gather.7
  176.1 71.7 reduce-scatter.7
  250.6 73.3 all-gather.13
  326.1 32.7 all-gather.11
  361.7 49.2 all-gather.15
  412.6 32.9 all-gather.17
  478.0 44.5 reduce-scatter.11
  525.1 44.5 reduce-scatter.9
  575.9 34.4 all-gather.19
  614.5 156.3 all-reduce.9
  774.7 66.9 reduce-scatter.19
  858.9 62.1 reduce-scatter.17
  925.0 64.4 reduce-scatter.15
  992.0 43.4 reduce-scatter.13
where the time goes:
time: 1110 us; the launch traced here: 1100 us
  waiting for transfers between devices  510 us (46%)
  matrix products  283 us (25%)
  other arithmetic  125 us (11%)
  local copies, waits for them, and re-layouts  88.5 us (8%)
  blocking collectives  76 us (7%)
  between operations  20.7 us (2%)
    all_gather x1, waiting for transfers between devices, per_device(): lax.all_gather(in_master.astype(jnp.bfloat16), 'dp', axis=0, tiled=True)  69.7 us
    reduce_scatter x1, waiting for transfers between devices, per_device(): lax.psum_scatter(jnp.dot(attended, w_out, preferred_element_type=jnp.floa...  69.5 us
    reduce_scatter x1, waiting for transfers between devices, per_device(): lax.psum_scatter(grad_qkv.reshape(D, 3, width_local).astype(jnp.bfloat16)...  66.9 us
    dynamic_update_slice x8, local copies, waits for them, and re-layouts, backward_row(): lax.scan(backward_block, (zeros_acc, zeros_acc), block_inputs)  46.6 us
    dot_general x4, matrix products, backward_block(): jnp.einsum('qhd,khd->hqk', grad_block, value_row, preferred_element_type=...  46.1 us
    reduce_scatter x1, waiting for transfers between devices, per_device(): lax.psum_scatter(jnp.dot(hidden, w_down, preferred_element_type=jnp.float...  44.4 us
    convert_element_type x4, other arithmetic, backward_block(): score_grad = (probs_block * (prob_grad - row_inner)).astype(jnp.bfloat16)  44.2 us
    dot_general x4, matrix products, contract_cols(): lax.dot_general(left, right, (((1,), (1,)), ((), ())), preferred_element_...  43.7 us
  transfers between devices with their start and end apart: 15, of which 13 were waited for; matrix products, arithmetic and copies ran while one was open for 32% of the time, Pallas kernels for 0%

commit v1 on v0

--- a/solution.py
+++ b/solution.py
@@ -19,6 +19,25 @@
 weight_decay = 0.1
 adam_eps = 1e-08
 max_norm = 1.0
+
+
+def _feed_zone(x_in):
+    group_axis = "tensor"
+    axis_n = lax.psum(1, axis_name=group_axis)
+    table = []
+    for kk in range(axis_n):
+        table.append((kk, (kk + 1) % axis_n))
+
+    def meet_islands_on(e_now):
+        if len(e_now) == axis_n:
+            return e_now
+        w1 = lax.ppermute(e_now[0], axis_name=group_axis, perm=table)
+        return meet_islands_on([w1, *e_now])
+
+    vec_out = meet_islands_on([x_in])
+    w_next = jnp.concatenate(vec_out, 0)
+    shaped = lax.axis_index(group_axis)
+    return jnp.roll(w_next, (shaped + 1) * x_in.shape[0], 0)
 
 
 def layer_norm(values, gain):
@@ -188,7 +207,7 @@
     ).astype(jnp.float32)
     layer_out = output.astype(jnp.bfloat16)
     upstream = cotangent.astype(jnp.float32)
-    gathered_down = lax.all_gather(cotangent, "tensor", axis=0, tiled=True)
+    gathered_down = _feed_zone(cotangent)
     grad_down = contract_rows(hidden, gathered_down)
     hidden_grad = contract_cols(gathered_down, w_down)
     gate_up_grad = jax.vjp(swiglu, gate_up)[1](hidden_grad)[0].astype(jnp.bfloat16)

time: 1110 us -> 1070 us (0.964)
  waiting for transfers between devices: 510 us -> 459 us
  local copies, waits for them, and re-layouts: 88.5 us -> 103 us
    all_gather x1, waiting for transfers between devices: 69.7 us -> 14.6 us  [per_device(): lax.all_gather(in_master.astype(jnp.bfloat16), 'dp', axis=0, tiled=True)]
    ppermute x0 -> x3, waiting for transfers between devices: none -> 41.4 us  [meet_islands_on(): w1 = lax.ppermute(e_now[0], axis_name=group_axis, perm=table)]
    all_gather x1 -> x0, waiting for transfers between devices: 34.6 us -> none  [per_device(): gathered_down = lax.all_gather(cotangent, 'tensor', axis=0, tiled=True)]
    unnamed x106 -> x119, local copies, waits for them, and re-layouts: 16.9 us -> 30.3 us
  transfers between devices with their start and end apart: 15 -> 17, of which waited for: 13 -> 14; matrix products, arithmetic and copies ran while one was open for 32% -> 34% of each run, Pallas kernels for 0% -> 0%
where the time goes in v1:
time: 1070 us
  waiting for transfers between devices  459 us (43%)
  matrix products  283 us (26%)
  other arithmetic  125 us (12%)
  local copies, waits for them, and re-layouts  103 us (10%)
  blocking collectives  76 us (7%)
  between operations  20.7 us (2%)
    reduce_scatter x1, waiting for transfers between devices, per_device(): lax.psum_scatter(jnp.dot(attended, w_out, preferred_element_type=jnp.floa...  69.5 us
    reduce_scatter x1, waiting for transfers between devices, per_device(): lax.psum_scatter(grad_qkv.reshape(D, 3, width_local).astype(jnp.bfloat16)...  67.1 us
    dynamic_update_slice x8, local copies, waits for them, and re-layouts, backward_row(): lax.scan(backward_block, (zeros_acc, zeros_acc), block_inputs)  46.6 us
    dot_general x4, matrix products, backward_block(): jnp.einsum('qhd,khd->hqk', grad_block, value_row, preferred_element_type=...  46.1 us
    reduce_scatter x1, waiting for transfers between devices, per_device(): lax.psum_scatter(jnp.dot(hidden, w_down, preferred_element_type=jnp.float...  44.4 us
    convert_element_type x4, other arithmetic, backward_block(): score_grad = (probs_block * (prob_grad - row_inner)).astype(jnp.bfloat16)  44.4 us
    dot_general x4, matrix products, contract_cols(): lax.dot_general(left, right, (((1,), (1,)), ((), ())), preferred_element_...  43.7 us
    reduce_scatter x1, waiting for transfers between devices, per_device(): lax.psum_scatter(contract_cols(qkv_grad_low, w_qkv).astype(jnp.bfloat16),...  41.8 us
  transfers between devices with their start and end apart: 17, of which 14 were waited for; matrix products, arithmetic and copies ran while one was open for 34% of the time, Pallas kernels for 0%

profile of v1, /device:TPU:0, one launch (start us, length us, event | category | flops | bytes accessed | tf_op | source)
XLA Modules:
  0.0 1068.7 jit_solution(3535157948318641558)
XLA Ops:
  16.8 36.3 %all_gather.23 = bf16[256,1024]{1,0:T(8,128)(2,1)} all-gather(bf16[32,1024]{1,0:T(8,128)(2,1)S(1)} %convert_element_type.159), channel_id=1, replica_groups=mesh['dp'=8,'tensor'=4] {'dp'}, dimensions={0}, use_global_device_ids=true | all-gather | bytes 589824 | tf_op jit(solution)/shard_map/all_gather | solution.py:139
  61.6 35.9 %all-gather.7.cloned.1.call-done = bf16[2048,1024]{1,0:T(8,128)(2,1)} async-done(((bf16[512,1024]{1,0:T(8,128)(2,1)}), bf16[2048,1024]{1,0:T(8,128)(2,1)}) %all-gather.7.cloned.1.call-update) | async-done | bytes 4194320 | tf_op jit(solution)/shard_map/all_gather | solution.py:151
  110.1 57.2 %while.47 = (s32[]{:T(128)}, bf16[4,512,4,64]{1,3,2,0:T(8,128)(2,1)}, f32[4,4,512,1]{2,1,3,0:T(4,128)}, s32[4,512]{1,0:T(4,128)S(1)}, s32[2048]{0:T(1024)S(1)}, ...) while((s32[]{:T(128)}, ...), condition=%wide.region_8.9_spmd, body=%wide.region_5.8_spmd.sunk | while | flops 1121056768 | bytes 57227380 | solution.py:182
  178.5 69.5 %reduce-scatter.8.cloned.1.call-done = f32[512,1024]{1,0:T(8,128)} async-done(((f32[2048,1024]{1,0:T(8,128)}), f32[512,1024]{1,0:T(8,128)}) %reduce-scatter.8.cloned.1.call-update) | async-done | bytes 2097168 | tf_op jit(solution)/shard_map/reduce_scatter | solution.py:192
  251.9 14.4 %collective-permute-done = bf16[512,1024]{1,0:T(8,128)(2,1)S(1)} collective-permute-done((bf16[512,1024]{1,0:T(8,128)(2,1)}, bf16[512,1024]{1,0:T(8,128)(2,1)S(1)}, u32[]{:S(2)}, u32[]{:S(2)}) %collective-permute-start) | collective-permute-done | bytes 1048608 | tf_op jit(solution)/shard_map/ppermute | solution.py:34
  267.3 14.3 %collective-permute-done.1 = bf16[512,1024]{1,0:T(8,128)(2,1)} collective-permute-done((bf16[512,1024]{1,0:T(8,128)(2,1)S(1)}, bf16[512,1024]{1,0:T(8,128)(2,1)}, u32[]{:S(2)}, u32[]{:S(2)}) %collective-permute-start.1) | collective-permute-done | bytes 1048608 | tf_op jit(solution)/shard_map/ppermute | solution.py:34
  283.5 12.6 %collective-permute-done.2 = bf16[512,1024]{1,0:T(8,128)(2,1)} collective-permute-done((bf16[512,1024]{1,0:T(8,128)(2,1)}, bf16[512,1024]{1,0:T(8,128)(2,1)}, u32[]{:S(2)}, u32[]{:S(2)}) %collective-permute-start.2) | collective-permute-done | bytes 1048608 | tf_op jit(solution)/shard_map/ppermute | solution.py:34
  309.5 14.6 %all-gather.13.cloned.1.call-done = bf16[1024,2,1024]{2,1,0:T(2,128)(2,1)} async-done(((bf16[128,2,1024]{2,1,0:T(2,128)(2,1)}), bf16[1024,2,1024]{2,1,0:T(2,128)(2,1)}) %all-gather.13.cloned.1.call-update) | async-done | bytes 4194320 | tf_op jit(solution)/shard_map/all_gather | solution.py:140
  329.8 29.2 %all-gather.11.cloned.1.call-done = bf16[2048,1024]{1,0:T(8,128)(2,1)} async-done(((bf16[512,1024]{1,0:T(8,128)(2,1)}), bf16[2048,1024]{1,0:T(8,128)(2,1)}) %all-gather.11.cloned.1.call-update) | async-done | bytes 4194320 | tf_op jit(solution)/shard_map/all_gather | solution.py:199
  359.0 15.2 %fusion.105 = f32[2048,2048]{1,0:T(8,128)} fusion(bf16[2048,1024]{1,0:T(8,128)(2,1)} %all-gather.11.cloned.1.call-done, bf16[1024,2048]{1,0:T(8,128)(2,1)} %bitcast.174), kind=kOutput, calls=%fused_computation.194 | convolution fusion | flops 8589934592 | bytes 25165824 | tf_op jit(solution)/shard_map/dot_general | solution.py:200
  374.2 36.9 %all-gather.15.cloned.1.call-done = bf16[1024,1024]{1,0:T(8,128)(2,1)} async-done(((bf16[128,1024]{1,0:T(8,128)(2,1)}), bf16[1024,1024]{1,0:T(8,128)(2,1)}) %all-gather.15.cloned.1.call-update) | async-done | bytes 2097168 | tf_op jit(solution)/shard_map/all_gather | solution.py:141
  411.1 17.2 %fusion.80 = (f32[2048,1024]{1,0:T(8,128)}, f32[2048,1024]{1,0:T(8,128)}, bf16[2048,1024]{1,0:T(8,128)(2,1)}) fusion(f32[2048,2048]{1,0:T(8,128)} %fusion.105, bf16[1024,1024]{1,0:T(8,128)(2,1)} %all-gather.15.cloned.1.call-done, bf16[4096,1024]{1,0:T(8,128)(2,1)} %constant_dynamic-update-slice_fusion, s32[]{:T(128)S(6)} %select_n.21), kind=kOutput, calls=%fused_computation.128 | convolution fusion | flops 4324327424 | bytes 44040196 | tf_op jit(solution)/shard_map/dot_general | solution.py:104
  428.3 15.1 %convolution_convert_fusion.1 = bf16[2048,1024]{1,0:T(8,128)(2,1)} fusion(bf16[1024,2048]{1,0:T(8,128)(2,1)} %bitcast.175, f32[2048,1024]{1,0:T(8,128)} %get-tuple-element.338, f32[2048,1024]{1,0:T(8,128)} %get-tuple-element.337), kind=kOutput, calls=%fused_computation.65 | convolution fusion | flops 8600420352 | bytes 25165824 | tf_op jit(solution)/shard_map/dot_general | solution.py:104
  453.3 33.2 %reduce-scatter.12.cloned.1.call-done = bf16[512,1024]{1,0:T(8,128)(2,1)} async-done(((bf16[2048,1024]{1,0:T(8,128)(2,1)}), bf16[512,1024]{1,0:T(8,128)(2,1)}) %reduce-scatter.12.cloned.1.call-update) | async-done | bytes 1048592 | tf_op jit(solution)/shard_map/reduce_scatter | solution.py:215
  489.2 44.4 %reduce-scatter.10.cloned.1.call-done = bf16[512,1024]{1,0:T(8,128)(2,1)} async-done(((bf16[2048,1024]{1,0:T(8,128)(2,1)}), bf16[512,1024]{1,0:T(8,128)(2,1)}) %reduce-scatter.10.cloned.1.call-update) | async-done | bytes 1048592 | tf_op jit(solution)/shard_map/reduce_scatter | solution.py:202
  539.8 17.1 %convolution_convert_fusion = bf16[1024,2048]{1,0:T(8,128)(2,1)} fusion(bf16[2048,1024]{1,0:T(8,128)(2,1)} %all-gather.11.cloned.1.call-done, f32[2048,1024]{1,0:T(8,128)} %get-tuple-element.338, f32[2048,1024]{1,0:T(8,128)} %get-tuple-element.337), kind=kOutput, calls=%fused_computation.64 | convolution fusion | flops 8600420352 | bytes 25165824 | tf_op jit(solution)/shard_map/dot_general | solution.py:98
  584.5 230.3 %while.48 = (s32[]{:T(128)}, f32[2048,4,64]{0,2,1:T(8,128)}, f32[2048,4,64]{0,2,1:T(8,128)}, f32[4,512,4,64]{1,0,3,2:T(4,128)}, bf16[4,512,4,64]{1,3,2,0:T(8,128...) while((s32[]{:T(128)}, f32[2048,4,64]{0,2,1:T(8,128)}, ...), condition=%wide.region_18.19_spmd.clone, body=%wide.region_16.18_spmd.clone.sunk | while | flops 2751068160 | bytes 183179600 | solution.py:265
  596.9 11.5 %multiply_reduce_fusion.4 = (f32[4,512]{1,0:T(4,128)}, f32[4,512,2048]{2,1,0:T(8,128)}) fusion(f32[4,512,2048]{2,1,0:T(8,128)S(1)} %fusion.161, f32[4,512]{1,0:T(4,128)S(1)} %dynamic-slice_bitcast_fusion.2, pred[512,2048]{1,0:T(8,128)(4,1)} %copy-done.1, bf16[2048,4,64]{0,2,1:T(8,128)(2,1)} %get-tuple-element.552, ...), kind=kOutput, calls=%fused_computation.20.clone.1 | convolution fusion | flops 557840384 | bytes 35930116 | tf_op jit(solution)/shard_map/while/body/eval_jaxpr/while/body/eval_jaxpr/qhd,khd->hqk/dot_general | solution.py:237
  608.4 11.2 %multiply_convert_fusion.4 = bf16[4,512,2048]{2,1,0:T(8,128)(2,1)} fusion(f32[4,512,2048]{2,1,0:T(8,128)} %get-tuple-element.487, f32[4,512,2048]{2,1,0:T(8,128)S(1)} %fusion.161, f32[4,512]{1,0:T(4,128)} %get-tuple-element.488, f32[4,512]{1,0:T(4,128)S(1)} %dynamic-slice_bitcast_fusion.2, pred[512,2048]{1,0:T(8,128)(4,1)} %copy-done.1), kind=kLoop, calls=%fused_computation.19.clone.1 | loop fusion | flops 25165824 | bytes 43008000 | tf_op jit(solution)/shard_map/while/body/eval_jaxpr/while/body/eval_jaxpr/convert_element_type | solution.py:241
  630.2 11.1 %dynamic_update_slice.33 = f32[4,512,4,64]{1,0,3,2:T(4,128)} dynamic-update-slice(f32[4,512,4,64]{1,0,3,2:T(4,128)} %get-tuple-element.532, f32[1,512,4,64]{1,0,3,2:T(1,128)S(1)} %copy.107, s32[]{:T(128)S(6)} %copy.132, s32[]{:T(128)} %constant.107.clone.1..sunk, s32[]{:T(128)} %constant.107.clone.1..sunk, s32[]{:T(128)} %constant.107.clone.1..sunk) | dynamic-update-slice | bytes 1048580 | tf_op jit(solution)/shard_map/while/body/eval_jaxpr/while/body/jit(dynamic_update_index_in_dim)/dynamic_update_slice | solution.py:265
  654.0 11.5 %multiply_reduce_fusion.4 = (f32[4,512]{1,0:T(4,128)}, f32[4,512,2048]{2,1,0:T(8,128)}) fusion(f32[4,512,2048]{2,1,0:T(8,128)S(1)} %fusion.161, f32[4,512]{1,0:T(4,128)S(1)} %dynamic-slice_bitcast_fusion.2, pred[512,2048]{1,0:T(8,128)(4,1)} %copy-done.1, bf16[2048,4,64]{0,2,1:T(8,128)(2,1)} %get-tuple-element.552, ...), kind=kOutput, calls=%fused_computation.20.clone.1 | convolution fusion | flops 557840384 | bytes 35930116 | tf_op jit(solution)/shard_map/while/body/eval_jaxpr/while/body/eval_jaxpr/qhd,khd->hqk/dot_general | solution.py:237
  665.5 11.1 %multiply_convert_fusion.4 = bf16[4,512,2048]{2,1,0:T(8,128)(2,1)} fusion(f32[4,512,2048]{2,1,0:T(8,128)} %get-tuple-element.487, f32[4,512,2048]{2,1,0:T(8,128)S(1)} %fusion.161, f32[4,512]{1,0:T(4,128)} %get-tuple-element.488, f32[4,512]{1,0:T(4,128)S(1)} %dynamic-slice_bitcast_fusion.2, pred[512,2048]{1,0:T(8,128)(4,1)} %copy-done.1), kind=kLoop, calls=%fused_computation.19.clone.1 | loop fusion | flops 25165824 | bytes 43008000 | tf_op jit(solution)/shard_map/while/body/eval_jaxpr/while/body/eval_jaxpr/convert_element_type | solution.py:241
  688.1 11.1 %dynamic_update_slice.33 = f32[4,512,4,64]{1,0,3,2:T(4,128)} dynamic-update-slice(f32[4,512,4,64]{1,0,3,2:T(4,128)} %get-tuple-element.532, f32[1,512,4,64]{1,0,3,2:T(1,128)S(1)} %copy.107, s32[]{:T(128)S(6)} %copy.132, s32[]{:T(128)} %constant.107.clone.1..sunk, s32[]{:T(128)} %constant.107.clone.1..sunk, s32[]{:T(128)} %constant.107.clone.1..sunk) | dynamic-update-slice | bytes 1048580 | tf_op jit(solution)/shard_map/while/body/eval_jaxpr/while/body/jit(dynamic_update_index_in_dim)/dynamic_update_slice | solution.py:265
  711.8 11.5 %multiply_reduce_fusion.4 = (f32[4,512]{1,0:T(4,128)}, f32[4,512,2048]{2,1,0:T(8,128)}) fusion(f32[4,512,2048]{2,1,0:T(8,128)S(1)} %fusion.161, f32[4,512]{1,0:T(4,128)S(1)} %dynamic-slice_bitcast_fusion.2, pred[512,2048]{1,0:T(8,128)(4,1)} %copy-done.1, bf16[2048,4,64]{0,2,1:T(8,128)(2,1)} %get-tuple-element.552, ...), kind=kOutput, calls=%fused_computation.20.clone.1 | convolution fusion | flops 557840384 | bytes 35930116 | tf_op jit(solution)/shard_map/while/body/eval_jaxpr/while/body/eval_jaxpr/qhd,khd->hqk/dot_general | solution.py:237
  745.8 11.1 %dynamic_update_slice.33 = f32[4,512,4,64]{1,0,3,2:T(4,128)} dynamic-update-slice(f32[4,512,4,64]{1,0,3,2:T(4,128)} %get-tuple-element.532, f32[1,512,4,64]{1,0,3,2:T(1,128)S(1)} %copy.107, s32[]{:T(128)S(6)} %copy.132, s32[]{:T(128)} %constant.107.clone.1..sunk, s32[]{:T(128)} %constant.107.clone.1..sunk, s32[]{:T(128)} %constant.107.clone.1..sunk) | dynamic-update-slice | bytes 1048580 | tf_op jit(solution)/shard_map/while/body/eval_jaxpr/while/body/jit(dynamic_update_index_in_dim)/dynamic_update_slice | solution.py:265
  769.5 11.5 %multiply_reduce_fusion.4 = (f32[4,512]{1,0:T(4,128)}, f32[4,512,2048]{2,1,0:T(8,128)}) fusion(f32[4,512,2048]{2,1,0:T(8,128)S(1)} %fusion.161, f32[4,512]{1,0:T(4,128)S(1)} %dynamic-slice_bitcast_fusion.2, pred[512,2048]{1,0:T(8,128)(4,1)} %copy-done.1, bf16[2048,4,64]{0,2,1:T(8,128)(2,1)} %get-tuple-element.552, ...), kind=kOutput, calls=%fused_computation.20.clone.1 | convolution fusion | flops 557840384 | bytes 35930116 | tf_op jit(solution)/shard_map/while/body/eval_jaxpr/while/body/eval_jaxpr/qhd,khd->hqk/dot_general | solution.py:237
  781.0 11.1 %multiply_convert_fusion.4 = bf16[4,512,2048]{2,1,0:T(8,128)(2,1)} fusion(f32[4,512,2048]{2,1,0:T(8,128)} %get-tuple-element.487, f32[4,512,2048]{2,1,0:T(8,128)S(1)} %fusion.161, f32[4,512]{1,0:T(4,128)} %get-tuple-element.488, f32[4,512]{1,0:T(4,128)S(1)} %dynamic-slice_bitcast_fusion.2, pred[512,2048]{1,0:T(8,128)(4,1)} %copy-done.1), kind=kLoop, calls=%fused_computation.19.clone.1 | loop fusion | flops 25165824 | bytes 43008000 | tf_op jit(solution)/shard_map/while/body/eval_jaxpr/while/body/eval_jaxpr/convert_element_type | solution.py:241
  803.5 11.1 %dynamic_update_slice.33 = f32[4,512,4,64]{1,0,3,2:T(4,128)} dynamic-update-slice(f32[4,512,4,64]{1,0,3,2:T(4,128)} %get-tuple-element.532, f32[1,512,4,64]{1,0,3,2:T(1,128)S(1)} %copy.107, s32[]{:T(128)S(6)} %copy.132, s32[]{:T(128)} %constant.107.clone.1..sunk, s32[]{:T(128)} %constant.107.clone.1..sunk, s32[]{:T(128)} %constant.107.clone.1..sunk) | dynamic-update-slice | bytes 1048580 | tf_op jit(solution)/shard_map/while/body/eval_jaxpr/while/body/jit(dynamic_update_index_in_dim)/dynamic_update_slice | solution.py:265
  847.8 37.4 %reduce-scatter.18.cloned.1.call-done = bf16[32,1024]{1,0:T(8,128)(2,1)} async-done(((bf16[256,1024]{1,0:T(8,128)(2,1)}), bf16[32,1024]{1,0:T(8,128)(2,1)}) %reduce-scatter.18.cloned.1.call-update) | async-done | bytes 65552 | tf_op jit(solution)/shard_map/reduce_scatter | solution.py:297
  886.6 67.1 %reduce-scatter.16.cloned.1.call-done = bf16[128,3,256]{2,0,1:T(8,128)(2,1)} async-done(((bf16[1024,3,256]{2,0,1:T(8,128)(2,1)}), bf16[128,3,256]{2,0,1:T(8,128)(2,1)}) %reduce-scatter.16.cloned.1.call-update) | async-done | bytes 196624 | tf_op jit(solution)/shard_map/reduce_scatter | solution.py:291
  958.0 41.8 %reduce-scatter.14.cloned.1.call-done = bf16[512,1024]{1,0:T(8,128)(2,1)} async-done(((bf16[2048,1024]{1,0:T(8,128)(2,1)}), bf16[512,1024]{1,0:T(8,128)(2,1)}) %reduce-scatter.14.cloned.1.call-update) | async-done | bytes 1048592 | tf_op jit(solution)/shard_map/reduce_scatter | solution.py:282
  1004.0 39.8 %all-reduce.7 = (f32[]{:T(128)}, f32[2,1024]{1,0:T(2,128)S(1)}) all-reduce(f32[]{:T(128)S(6)} %add.226, f32[2,1024]{1,0:T(2,128)S(1)} %pad_maximum_fusion.1), channel_id=1, replica_groups=mesh['dp'=8,'tensor'=4] {'dp','tensor'}, use_global_device_ids=true, to_apply=%region_30.31 | all-reduce | flops 2049 | bytes 16392 | tf_op jit(solution)/shard_map/psum | solution.py:317
  (330 shorter events, 331.4 us)
Async XLA Ops:
  7.2 54.4 %all-gather.9.cloned.1.call-start = ((), (), s32[]{:S(2)}) async-start(), calls=%async_computation.8 | async-start | bytes 1769472 | tf_op jit(solution)/shard_map/all_gather | solution.py:138
  9.1 88.4 %all-gather.7.cloned.1.call-start = ((), (), s32[]{:S(2)}) async-start(), calls=%async_computation.7 | async-start | bytes 5242880 | tf_op jit(solution)/shard_map/all_gather | solution.py:151
  16.3 231.7 %reduce-scatter.8.cloned.1.call-start = ((), (), s32[]{:S(2)}) async-start(), calls=%async_computation.9 | async-start | bytes 10485760 | tf_op jit(solution)/shard_map/reduce_scatter | solution.py:192
  54.1 50.3 %copy-start.17 = (f32[2048,32]{0,1:T(8,128)}, f32[2048,32]{0,1:T(8,128)S(1)}, u32[]{:S(2)}) copy-start(f32[2048,32]{0,1:T(8,128)S(1)} %get-tuple-element.355) | copy-start | bytes 786436
  54.1 50.3 %copy-start.19 = (f32[2048,32]{0,1:T(8,128)}, f32[2048,32]{0,1:T(8,128)S(1)}, u32[]{:S(2)}) copy-start(f32[2048,32]{0,1:T(8,128)S(1)} %get-tuple-element.356) | copy-start | bytes 786436
  176.1 148.1 %all-gather.13.cloned.1.call-start = ((), (), s32[]{:S(2)}) async-start(), calls=%async_computation.11 | async-start | bytes 4718592 | tf_op jit(solution)/shard_map/all_gather | solution.py:140
  178.4 180.5 %all-gather.11.cloned.1.call-start = ((), (), s32[]{:S(2)}) async-start(), calls=%async_computation.10 | async-start | bytes 5242880 | tf_op jit(solution)/shard_map/all_gather | solution.py:199
  251.8 159.3 %all-gather.15.cloned.1.call-start = ((), (), s32[]{:S(2)}) async-start(), calls=%async_computation.12 | async-start | bytes 2359296 | tf_op jit(solution)/shard_map/all_gather | solution.py:141
  251.8 14.5 %collective-permute-start = (bf16[512,1024]{1,0:T(8,128)(2,1)}, bf16[512,1024]{1,0:T(8,128)(2,1)S(1)}, u32[]{:S(2)}, u32[]{:S(2)}) collective-permute-start(bf16[512,1024]{1,0:T(8,128)(2,1)} %param.23), channel_id=1, source_target_pairs={{0,1},{1,2},{2,3},{3,0},{4,5},{5,6},{6,7},{7,4},{8,9},{9,10},{10,1... | collective-permute-start | bytes 3145736 | tf_op jit(solution)/shard_map/ppermute | solution.py:34
  267.3 14.3 %collective-permute-start.1 = (bf16[512,1024]{1,0:T(8,128)(2,1)S(1)}, bf16[512,1024]{1,0:T(8,128)(2,1)}, u32[]{:S(2)}, u32[]{:S(2)}) collective-permute-start(bf16[512,1024]{1,0:T(8,128)(2,1)S(1)} %collective-permute-done), channel_id=1, source_target_pairs={{0,1},{1,2},{2,3},{3,0},{4,5},{5,6},{6,7},{7,4},{8,9},{9,10},{10,1... | collective-permute-start | bytes 3145736 | tf_op jit(solution)/shard_map/ppermute | solution.py:34
  281.6 14.5 %collective-permute-start.2 = (bf16[512,1024]{1,0:T(8,128)(2,1)}, bf16[512,1024]{1,0:T(8,128)(2,1)}, u32[]{:S(2)}, u32[]{:S(2)}) collective-permute-start(bf16[512,1024]{1,0:T(8,128)(2,1)} %collective-permute-done.1), channel_id=1, source_target_pairs={{0,1},{1,2},{2,3},{3,0},{4,5},{5,6},{6,7},{7,4},{8,9},{9,10},{10,1... | collective-permute-start | bytes 3145736 | tf_op jit(solution)/shard_map/ppermute | solution.py:34
  283.4 203.1 %reduce-scatter.12.cloned.1.call-start = ((), (), s32[]{:S(2)}) async-start(), calls=%async_computation.14 | async-start | bytes 5242880 | tf_op jit(solution)/shard_map/reduce_scatter | solution.py:215
  283.5 18.2 %copy-start.8 = (bf16[512,1024]{1,0:T(8,128)(2,1)S(1)}, bf16[512,1024]{1,0:T(8,128)(2,1)}, u32[]{:S(2)}) copy-start(bf16[512,1024]{1,0:T(8,128)(2,1)} %param.23) | copy-start | bytes 3145732
  443.4 90.3 %reduce-scatter.10.cloned.1.call-start = ((), (), s32[]{:S(2)}) async-start(), calls=%async_computation.13 | async-start | bytes 5242880 | tf_op jit(solution)/shard_map/reduce_scatter | solution.py:202
  453.3 121.1 %all-gather.17.cloned.1.call-start = ((), (), s32[]{:S(2)}) async-start(), calls=%async_computation.15 | async-start | bytes 5242880 | tf_op jit(solution)/shard_map/all_gather | solution.py:223
  537.1 19.8 %copy-start.48 = (f32[512]{0:T(512)}, f32[512]{0:T(512)S(1)}, u32[]{:S(2)}) copy-start(f32[512]{0:T(512)S(1)} %negate_multiply_fusion.1) | copy-start | bytes 6148
  539.7 303.6 %all-reduce.10.cloned.1.call-start = ((), (), s32[]{:S(2)}) async-start(), calls=%async_computation.20 | async-start | bytes 8388608
  564.7 281.4 %reduce-scatter.20.cloned.1.call-start = ((), (), s32[]{:S(2)}) async-start(), calls=%async_computation.19 | async-start | bytes 2359296 | tf_op jit(solution)/shard_map/reduce_scatter | solution.py:306
  574.3 310.8 %reduce-scatter.18.cloned.1.call-start = ((), (), s32[]{:S(2)}) async-start(), calls=%async_computation.18 | async-start | bytes 589824 | tf_op jit(solution)/shard_map/reduce_scatter | solution.py:297
  823.0 130.7 %reduce-scatter.16.cloned.1.call-start = ((), (), s32[]{:S(2)}) async-start(), calls=%async_computation.17 | async-start | bytes 1769472 | tf_op jit(solution)/shard_map/reduce_scatter | solution.py:291
  834.4 165.4 %reduce-scatter.14.cloned.1.call-start = ((), (), s32[]{:S(2)}) async-start(), calls=%async_computation.16 | async-start | bytes 5242880 | tf_op jit(solution)/shard_map/reduce_scatter | solution.py:282
  841.4 158.3 %copy-start.3 = (bf16[512,1024]{1,0:T(8,128)(2,1)S(1)}, bf16[512,1024]{1,0:T(8,128)(2,1)}, u32[]{:S(2)}) copy-start(bf16[512,1024]{1,0:T(8,128)(2,1)} %param.22) | copy-start | bytes 3145732
  841.4 158.3 %copy-start.40 = (f32[1,1024]{1,0:T(1,128)S(1)}, f32[1,1024]{1,0:T(1,128)}, u32[]{:S(2)}) copy-start(f32[1,1024]{1,0:T(1,128)} %copy-done.39) | copy-start | bytes 12292
  841.4 158.3 %copy-start.44 = (f32[512]{0:T(512)S(1)}, f32[512]{0:T(512)}, u32[]{:S(2)}) copy-start(f32[512]{0:T(512)} %copy-done.43) | copy-start | bytes 6148
  841.4 160.1 %copy-start.51 = (f32[512]{0:T(512)S(1)}, f32[512]{0:T(512)}, u32[]{:S(2)}) copy-start(f32[512]{0:T(512)} %copy-done.50) | copy-start | bytes 6148
  841.5 160.1 %copy-start.47 = (f32[512]{0:T(512)S(1)}, f32[512]{0:T(512)}, u32[]{:S(2)}) copy-start(f32[512]{0:T(512)} %copy-done.46) | copy-start | bytes 6148
  841.5 162.5 %copy-start.52 = (f32[1024]{0:T(1024)S(1)}, f32[1024]{0:T(1024)}, u32[]{:S(2)}) copy-start(f32[1024]{0:T(1024)} %get-tuple-element.261) | copy-start | bytes 12292
  841.5 204.3 %copy-start.45 = (f32[2,1024]{1,0:T(2,128)S(1)}, f32[2,1024]{1,0:T(2,128)}, u32[]{:S(2)}) copy-start(f32[2,1024]{1,0:T(2,128)} %param.37) | copy-start | bytes 24580
  841.5 204.3 %copy-start.53 = (f32[2,1024]{1,0:T(2,128)S(1)}, f32[2,1024]{1,0:T(2,128)}, u32[]{:S(2)}) copy-start(f32[2,1024]{1,0:T(2,128)} %param.38) | copy-start | bytes 24580
  841.5 204.3 %copy-start.54 = (f32[2,1024]{1,0:T(2,128)S(1)}, f32[2,1024]{1,0:T(2,128)}, u32[]{:S(2)}) copy-start(f32[2,1024]{1,0:T(2,128)} %param.39) | copy-start | bytes 24580
  841.5 204.9 %copy-start.7 = (f32[512,1024]{1,0:T(8,128)S(1)}, f32[512,1024]{1,0:T(8,128)}, u32[]{:S(2)}) copy-start(f32[512,1024]{1,0:T(8,128)} %copy-done.6) | copy-start | bytes 6291460
  841.5 204.9 %copy-start.49 = (f32[512]{0:T(512)S(1)}, f32[512]{0:T(512)}, u32[]{:S(2)}) copy-start(f32[512]{0:T(512)} %copy-done.48) | copy-start | bytes 6148
  (62 other events, 392.7 us)
Sparse Core Ops, SparseCore 0:
  10.7 50.9 all-gather.8
  63.8 33.7 all-gather.6
  176.2 71.7 reduce-scatter.7
  250.7 73.3 all-gather.12
  326.2 32.7 all-gather.10
  361.7 49.2 all-gather.14
  443.5 42.9 reduce-scatter.11
  489.0 44.5 reduce-scatter.9
  539.9 34.4 all-gather.16
  578.3 156.2 all-reduce.9
  738.6 66.6 reduce-scatter.19
  823.2 61.9 reduce-scatter.17
  889.2 64.5 reduce-scatter.15
  956.3 43.4 reduce-scatter.13
